TPU v7x, 32 devices: a whole 2x2x4 slice. The times are simulated.
32 devices in a mesh: replica: 2 (over core), shard: 16 (over z, y, x).
Axes of the slice: x: 2, y: 2, z: 4, core: 2. Of those that a mesh axis runs over, the one named last changes fastest.
Arguments:
- inner_params: bfloat16 [2, 15360, 4096], P('replica', 'shard'), may hold values from -6 to 6
- anchor: float32 [15360, 4096], P('shard'), may hold values from -6 to 6
- momentum: float32 [15360, 4096], P('shard'), may hold values from -2 to 2
- first_moment: bfloat16 [2, 15360, 4096], P('replica', 'shard'), may hold values from -0.59765625 to 0.59765625
- second_moment: bfloat16 [2, 15360, 4096], P('replica', 'shard'), may hold values from 0.0009994507 to 0.099609375
- activations: bfloat16 [2, 64, 4096], P('replica', 'shard'), may hold values from -6 to 6
- cotangent: bfloat16 [2, 15360, 64], P('replica', 'shard'), may hold values from -6 to 6
- spare_index: int32 [16], P('shard'), may hold values from 0 to 1
- peer_index: int32 [16], P('shard'), may hold values from 0 to 1
Outputs:
- anchor_new: float32 [15360, 4096], P('shard')
- momentum_new: float32 [15360, 4096], P('shard')
- update: float32 [2, 15360, 4096], P('replica', 'shard')
Inputs may be any that keep to these rules, and one draw needn't show every extreme that they name: `spare_index`: a replica index for each block. `peer_index`: a replica index for each block; where it equals spare_index the spare keeps its own moments.
All inputs are finite; a program needn't handle non-finite values.
Results may differ from a plain program's by a relative error of at most 0.0018.
Values may be sent and summed in bfloat16 or wider, within the bound.
No kernel may reach another device: no remote copies, remote signals or barrier semaphores. Data moves between devices by JAX's collectives and lax.ppermute only.
A program may use at most 192 MiB of HBM per device.

v0:
```python
import math
import jax
import jax.numpy as jnp
from jax import lax
from jax.sharding import PartitionSpec as P

outer_rate = 0.7
nesterov_mu = 0.9
beta_one = 0.9
beta_two = 0.95
bias_one = 1.0 - 0.9**40
bias_two = 1.0 - 0.95**40
adam_eps = 1e-08
decay_rate = 0.1


def from_root(block, axis, holder):
    block = jnp.where(lax.axis_index(axis) == holder, block, jnp.zeros_like(block))
    return lax.psum(block, axis)


def slope(pre):
    sigma = jax.nn.sigmoid(pre)
    return sigma * (1.0 + pre * (1.0 - sigma))


def local(
    inner_params,
    anchor,
    momentum,
    first_moment,
    second_moment,
    activations,
    cotangent,
    spare_index,
    peer_index,
):
    replicas = lax.axis_size("replica")
    position = lax.axis_index("replica")
    spare_slot = spare_index[0]
    peer_slot = peer_index[0]
    healthy = (position != spare_slot).astype(jnp.float32)
    difference = (anchor - inner_params[0].astype(jnp.float32)) * healthy
    summed = lax.psum(difference, "replica")
    average = summed / (replicas - 1)
    momentum_new = nesterov_mu * momentum + average
    anchor_new = anchor - outer_rate * (average + nesterov_mu * momentum_new)
    received = (
        from_root(first_moment, "replica", peer_slot),
        from_root(second_moment, "replica", peer_slot),
    )
    is_spare = position == spare_slot
    first_used = jnp.where(is_spare, received[0], first_moment)[0].astype(jnp.float32)
    second_used = jnp.where(is_spare, received[1], second_moment)[0].astype(jnp.float32)
    weights = anchor_new.astype(jnp.bfloat16)
    root = math.sqrt(weights.shape[1])
    cot_local = cotangent[0]
    tokens_part = lax.all_gather(activations, "shard", axis=1, tiled=True)[0]
    pre = (
        lax.dot_general(
            weights, tokens_part, (((1,), (1,)), ((), ())), preferred_element_type=jnp.float32
        )
        / root
    )
    grad_pre = (cot_local.astype(jnp.float32) * slope(pre)).astype(jnp.bfloat16)
    gradient = jnp.dot(grad_pre, tokens_part, preferred_element_type=jnp.float32) / root
    first = beta_one * first_used + (1.0 - beta_one) * gradient
    second = beta_two * second_used + (1.0 - beta_two) * gradient * gradient
    update = first / bias_one / (jnp.sqrt(second / bias_two) + adam_eps) + decay_rate * anchor_new
    return (anchor_new, momentum_new, update[None])


def solution(mesh):
    placed = (
        P("replica", "shard", None),
        P("shard", None),
        P("shard", None),
        P("replica", "shard", None),
        P("replica", "shard", None),
        P("replica", "shard", None),
        P("replica", "shard", None),
        P("shard"),
        P("shard"),
    )
    return jax.shard_map(
        local,
        mesh=mesh,
        in_specs=placed,
        out_specs=(P("shard", None), P("shard", None), P("replica", "shard", None)),
        check_vma=False,
    )
```

profile of v0, /device:TPU:0, one launch (start us, length us, event | category | flops | bytes accessed | tf_op | source)
XLA Modules:
  0.0 182.1 jit_solution(2626076116855206710)
XLA Ops:
  7.2 0.0 all-reduce.4.cloned.1.call-start
  7.9 13.2 %fusion = f32[960,4096]{1,0:T(8,128)} fusion(f32[960,4096]{1,0:T(8,128)} %param.10, bf16[1,960,4096]{2,1,0:T(8,128)(2,1)} %param.9, f32[]{:T(128)S(6)} %convert_element_type.31), kind=kLoop, calls=%fused_computation.1 | loop fusion | flops 11796480 | bytes 39321604 | tf_op jit(solution)/shard_map/mul | solution.py:43
  21.1 0.0 all-reduce.4.cloned.1.call-update
  21.1 0.0 all-reduce.6.cloned.1.call-start
  21.8 5.7 %broadcast_select_fusion = (bf16[1,960,4096]{2,1,0:T(8,128)(2,1)}, bf16[1,960,4096]{2,1,0:T(8,128)(2,1)}) fusion(bf16[1,960,4096]{2,1,0:T(8,128)(2,1)} %param.13, pred[]{:T(512)S(6)} %eq.8, bf16[1,960,4096]{2,1,0:T(8,128)(2,1)} %param.12), kind=kLoop, calls=%fused_computation.15 | loop fusion | flops 7864320 | bytes 31457280 | tf_op jit(solution)/shard_map/jit(_where)/select_n | solution.py:18
  27.5 0.0 copy-start
  27.5 0.0 all-reduce.6.cloned.1.call-update
  27.6 0.7 copy-done
  28.3 0.1 copy.13
  28.4 57.0 %all_gather.3 = bf16[1,64,4096]{2,0,1:T(2,128)(2,1)S(1)} all-gather(bf16[1,4,4096]{2,0,1:T(2,128)(2,1)S(1)} %copy.13), channel_id=1, replica_groups=mesh['replica'=2,'shard'=16] {'shard'}, dimensions={1}, use_global_device_ids=true | all-gather | bytes 557056 | tf_op jit(solution)/shard_map/all_gather | solution.py:58
  85.3 0.0 copy-start.1
  85.3 0.0 all-reduce.4.cloned.1.call-done
  85.3 32.9 %multiply_subtract_fusion = (f32[960,4096]{1,0:T(8,128)}, f32[960,4096]{1,0:T(8,128)}) fusion(f32[960,4096]{1,0:T(8,128)} %param.10, f32[960,4096]{1,0:T(8,128)} %all-reduce.4.cloned.1.call-done, f32[960,4096]{1,0:T(8,128)} %param.11), kind=kLoop, calls=%fused_computation.11 | loop fusion | flops 23592960 | bytes 78643200 | tf_op jit(solution)/shard_map/sub | solution.py:47
  118.2 21.2 %all-reduce.6.cloned.1.call-done = (bf16[1,960,4096]{2,1,0:T(8,128)(2,1)}, bf16[1,960,4096]{2,1,0:T(8,128)(2,1)}) async-done(((bf16[1,960,4096]{2,1,0:T(8,128)(2,1)}, bf16[1,960,4096]{2,1,0:T(8,128)(2,1)}), (bf16[1,960,4096]{2,1,0:T(8,128)(2,1)}, bf16[1,960,4096]{2,1,0:T(8,128)(2,1)})) %all-reduce.6.cloned.1.call-update) | async-done | bytes 15728656 | tf_op jit(solution)/shard_map/psum | solution.py:19
  139.5 0.0 copy-done.1
  139.5 35.8 %fusion.6 = f32[1,960,4096]{2,1,0:T(8,128)} fusion(f32[960,4096]{1,0:T(8,128)} %get-tuple-element.5, bf16[1,960,4096]{2,1,0:T(8,128)(2,1)} %get-tuple-element.3, bf16[1,960,4096]{2,1,0:T(8,128)(2,1)} %param.13, bf16[1,960,4096]{2,1,0:T(8,128)(2,1)} %get-tuple-element.4, bf16[1,960,4096]{2,1,0:T(8,128)(2,1)} %param.12, pred[]{:T(512)S(6)} %eq.7, ...), kind=kOutput, calls=%fused_computation.8 | convolution fusion | flops 1082019840 | bytes 63561728 | tf_op jit(solution)/shard_map/dot_general | solution.py:66
Async XLA Ops:
  7.2 78.2 %all-reduce.4.cloned.1.call-start = ((), (), s32[]{:S(2)}) async-start(), calls=%async_computation | async-start | bytes 31457280 | tf_op jit(solution)/shard_map/psum | solution.py:44
  21.1 118.4 %all-reduce.6.cloned.1.call-start = ((), (), s32[]{:S(2)}) async-start(), calls=%async_computation.1 | async-start | bytes 31457280 | tf_op jit(solution)/shard_map/psum | solution.py:19
  27.5 0.8 copy-start
  85.3 54.1 %copy-start.1 = (bf16[1,960,64]{1,2,0:T(8,128)(2,1)S(1)}, bf16[1,960,64]{1,2,0:T(8,128)(2,1)}, u32[]{:S(2)}) copy-start(bf16[1,960,64]{1,2,0:T(8,128)(2,1)} %param.15) | copy-start | bytes 368644
Sparse Core Ops, SparseCore 0:
  21.2 58.5 all-reduce.3
  82.4 57.0 all-reduce.5
where the time goes:
time: 182 us
  blocking collectives  57 us (31%)
  other arithmetic  51.9 us (29%)
  matrix products  35.8 us (20%)
  waiting for transfers between devices  21.3 us (12%)
  between operations  15.4 us (8%)
    all_gather x1, blocking collectives, local(): tokens_part = lax.all_gather(activations, 'shard', axis=1, tiled=True)[0]  57 us
    dot_general x1, matrix products, local(): jnp.dot(grad_pre, tokens_part, preferred_element_type=jnp.float32) / root  35.8 us
    sub x1, other arithmetic, local(): anchor_new = anchor - outer_rate * (average + nesterov_mu * momentum_new)  32.9 us
    psum x1, waiting for transfers between devices, from_root(): return lax.psum(block, axis)  21.2 us
    mul x1, other arithmetic, local(): difference = (anchor - inner_params[0].astype(jnp.float32)) * healthy  13.2 us
    select_n x1, other arithmetic, from_root(): jnp.where(lax.axis_index(axis) == holder, block, jnp.zeros_like(block))  5.75 us
  transfers between devices with their start and end apart: 2, of which 1 were waited for; matrix products, arithmetic and copies ran while one was open for 21% of the time, Pallas kernels for 0%

commit v1 on v0

--- a/solution.py
+++ b/solution.py
@@ -1,3 +1,4 @@
+import functools
 import math
 import jax
 import jax.numpy as jnp
@@ -12,6 +13,13 @@
 bias_two = 1.0 - 0.95**40
 adam_eps = 1e-08
 decay_rate = 0.1
+
+
+def resolve_slot(field_in, along_dim):
+    return jnp.concatenate(jax.lax.all_gather(field_in, axis_name="shard"), along_dim)
+
+
+push_rounds = functools.partial(resolve_slot, along_dim=1)
 
 
 def from_root(block, axis, holder):
@@ -55,7 +63,7 @@
     weights = anchor_new.astype(jnp.bfloat16)
     root = math.sqrt(weights.shape[1])
     cot_local = cotangent[0]
-    tokens_part = lax.all_gather(activations, "shard", axis=1, tiled=True)[0]
+    tokens_part = push_rounds(activations)[0]
     pre = (
         lax.dot_general(
             weights, tokens_part, (((1,), (1,)), ((), ())), preferred_element_type=jnp.float32

time: 182 us -> 182 us (level)
  waiting for transfers between devices: 21.3 us -> 25.9 us
  blocking collectives: 57 us -> 53.1 us
    psum x1, waiting for transfers between devices: 21.2 us -> 25.9 us  [from_root(): return lax.psum(block, axis)]
    all_gather x1, blocking collectives: 57 us -> 53.1 us  [resolve_slot(): jax.lax.all_gather(field_in, axis_name='shard')]
where the time goes in v1:
time: 182 us; the launch traced here: 181 us
  blocking collectives  53.1 us (29%)
  other arithmetic  50.9 us (28%)
  matrix products  35.2 us (19%)
  waiting for transfers between devices  25.9 us (14%)
  between operations  15.4 us (8%)
    all_gather x1, blocking collectives, resolve_slot(): jax.lax.all_gather(field_in, axis_name='shard')  53.1 us
    dot_general x1, matrix products, local(): jnp.dot(grad_pre, tokens_part, preferred_element_type=jnp.float32) / root  35.2 us
    sub x1, other arithmetic, local(): anchor_new = anchor - outer_rate * (average + nesterov_mu * momentum_new)  32 us
    psum x1, waiting for transfers between devices, from_root(): return lax.psum(block, axis)  25.9 us
    mul x1, other arithmetic, local(): difference = (anchor - inner_params[0].astype(jnp.float32)) * healthy  13.2 us
    select_n x1, other arithmetic, from_root(): jnp.where(lax.axis_index(axis) == holder, block, jnp.zeros_like(block))  5.75 us
  transfers between devices with their start and end apart: 2, of which 1 were waited for; matrix products, arithmetic and copies ran while one was open for 21% of the time, Pallas kernels for 0%

profile of v1, /device:TPU:0, one launch (start us, length us, event | category | flops | bytes accessed | tf_op | source)
XLA Modules:
  0.0 181.5 jit_solution(2473547470315777378)
XLA Ops:
  7.2 0.0 all-reduce.4.cloned.1.call-start
  7.9 13.2 %fusion = f32[960,4096]{1,0:T(8,128)} fusion(f32[960,4096]{1,0:T(8,128)} %param.10, bf16[1,960,4096]{2,1,0:T(8,128)(2,1)} %param.9, f32[]{:T(128)S(6)} %convert_element_type.31), kind=kLoop, calls=%fused_computation.1 | loop fusion | flops 11796480 | bytes 39321604 | tf_op jit(solution)/shard_map/mul | solution.py:51
  21.1 0.0 all-reduce.4.cloned.1.call-update
  21.1 0.0 all-reduce.6.cloned.1.call-start
  21.8 5.7 %broadcast_select_fusion = (bf16[1,960,4096]{2,1,0:T(8,128)(2,1)}, bf16[1,960,4096]{2,1,0:T(8,128)(2,1)}) fusion(bf16[1,960,4096]{2,1,0:T(8,128)(2,1)} %param.13, pred[]{:T(512)S(6)} %eq.8, bf16[1,960,4096]{2,1,0:T(8,128)(2,1)} %param.12), kind=kLoop, calls=%fused_computation.15 | loop fusion | flops 7864320 | bytes 31457280 | tf_op jit(solution)/shard_map/jit(_where)/select_n | solution.py:26
  27.5 0.0 copy-start
  27.5 0.0 all-reduce.6.cloned.1.call-update
  27.6 0.7 copy-done
  28.3 53.1 %all-gather = bf16[16,4,4096]{2,1,0:T(4,128)(2,1)S(1)} all-gather(bf16[1,4,4096]{2,1,0:T(4,128)(2,1)S(1)} %copy-done), channel_id=2, replica_groups=mesh['replica'=2,'shard'=16] {'shard'}, dimensions={0}, use_global_device_ids=true | all-gather | bytes 557056 | tf_op jit(solution)/shard_map/all_gather | solution.py:19
  81.4 0.1 squeeze_reshape.3
  81.5 0.0 copy-start.1
  81.6 0.0 all-reduce.4.cloned.1.call-done
  81.6 32.0 %multiply_subtract_fusion = (f32[960,4096]{1,0:T(8,128)}, f32[960,4096]{1,0:T(8,128)}) fusion(f32[960,4096]{1,0:T(8,128)} %param.10, f32[960,4096]{1,0:T(8,128)} %all-reduce.4.cloned.1.call-done, f32[960,4096]{1,0:T(8,128)} %param.11), kind=kLoop, calls=%fused_computation.11 | loop fusion | flops 23592960 | bytes 78643200 | tf_op jit(solution)/shard_map/sub | solution.py:55
  113.6 25.9 %all-reduce.6.cloned.1.call-done = (bf16[1,960,4096]{2,1,0:T(8,128)(2,1)}, bf16[1,960,4096]{2,1,0:T(8,128)(2,1)}) async-done(((bf16[1,960,4096]{2,1,0:T(8,128)(2,1)}, bf16[1,960,4096]{2,1,0:T(8,128)(2,1)}), (bf16[1,960,4096]{2,1,0:T(8,128)(2,1)}, bf16[1,960,4096]{2,1,0:T(8,128)(2,1)})) %all-reduce.6.cloned.1.call-update) | async-done | bytes 15728656 | tf_op jit(solution)/shard_map/psum | solution.py:27
  139.5 0.0 copy-done.1
  139.5 35.2 %fusion.6 = f32[1,960,4096]{2,1,0:T(8,128)} fusion(f32[960,4096]{1,0:T(8,128)} %get-tuple-element.5, bf16[1,960,4096]{2,1,0:T(8,128)(2,1)} %get-tuple-element.3, bf16[1,960,4096]{2,1,0:T(8,128)(2,1)} %param.13, bf16[1,960,4096]{2,1,0:T(8,128)(2,1)} %get-tuple-element.4, bf16[1,960,4096]{2,1,0:T(8,128)(2,1)} %param.12, pred[]{:T(512)S(6)} %eq.7, ...), kind=kOutput, calls=%fused_computation.8 | convolution fusion | flops 1082019840 | bytes 63561728 | tf_op jit(solution)/shard_map/dot_general | solution.py:74
Async XLA Ops:
  7.2 74.4 %all-reduce.4.cloned.1.call-start = ((), (), s32[]{:S(2)}) async-start(), calls=%async_computation | async-start | bytes 31457280 | tf_op jit(solution)/shard_map/psum | solution.py:52
  21.1 118.4 %all-reduce.6.cloned.1.call-start = ((), (), s32[]{:S(2)}) async-start(), calls=%async_computation.1 | async-start | bytes 31457280 | tf_op jit(solution)/shard_map/psum | solution.py:27
  27.5 0.8 copy-start
  81.5 57.9 %copy-start.1 = (bf16[1,960,64]{1,2,0:T(8,128)(2,1)S(1)}, bf16[1,960,64]{1,2,0:T(8,128)(2,1)}, u32[]{:S(2)}) copy-start(bf16[1,960,64]{1,2,0:T(8,128)(2,1)} %param.15) | copy-start | bytes 368644
Sparse Core Ops, SparseCore 0:
  21.2 58.5 all-reduce.3
  82.4 57.0 all-reduce.5
